TPU v7x, 32 devices: a whole 2x2x4 slice. The times are simulated.
32 devices in a mesh: rows: 4 (over z), vars: 8 (over y, x, core).
Axes of the slice: x: 2, y: 2, z: 4, core: 2. Of those that a mesh axis runs over, the one named last changes fastest.
Arguments:
- matrix: float32 [4096, 16384], P('rows', 'vars'), may hold values from -0.4 to 0.4
- barrier: float32 [16384], P('vars'), may hold values from 0.05 to 20
- panel_index: int32 [1], replicated, may hold values from 0 to 3
- row_offset: int32 [1], replicated, may hold values from 0 to 511
Outputs:
- factor_rows: float32 [4096, 512], P(('rows', 'vars'))
All inputs are finite; a program needn't handle non-finite values.
Results may differ from a plain program's by a relative error of at most 0.000092.
Values sent between devices are 32-bit elements; how exact they have to be, the bound alone decides.
A program may use at most 64 MiB of HBM per device.

v0:
```python
import jax
import jax.numpy as jnp
from jax import lax
from jax.sharding import PartitionSpec as P

PANEL = 512


def body(matrix, barrier, panel_index, row_offset):
    rows_here = matrix.shape[0]
    share_rows = rows_here // lax.axis_size("vars")
    first = panel_index[0] * PANEL + row_offset[0]
    own_first = lax.axis_index("rows") * rows_here
    wanted = first + jnp.arange(PANEL, dtype=jnp.int32)
    inside = (wanted >= own_first) & (wanted < own_first + rows_here)
    located = jnp.clip(wanted - own_first, 0, rows_here - 1)
    picked = jnp.take(matrix, located, axis=0) * inside[:, None].astype(jnp.float32)
    panel_rows = lax.psum(picked, "rows")
    scaled = panel_rows * barrier[None, :]
    vars_first = lax.axis_index("vars") * share_rows
    whole_sum = lax.psum(
        lax.dot_general(
            matrix,
            scaled,
            (((1,), (1,)), ((), ())),
            precision=lax.Precision.HIGHEST,
            preferred_element_type=jnp.float32,
        ),
        "vars",
    )
    normal_rows = lax.dynamic_slice_in_dim(whole_sum, vars_first, share_rows, 0)
    global_rows = own_first + vars_first + jnp.arange(share_rows, dtype=jnp.int32)
    col_ids = jnp.arange(PANEL, dtype=jnp.int32)
    normal_rows = normal_rows + (global_rows[:, None] == first + col_ids[None, :]).astype(
        jnp.float32
    )
    identity = jnp.eye(PANEL, dtype=jnp.float32)
    local_block = lax.dot_general(
        panel_rows,
        scaled,
        (((1,), (1,)), ((), ())),
        precision=lax.Precision.HIGHEST,
        preferred_element_type=jnp.float32,
    )
    diag_block = lax.psum(local_block, "vars") + identity
    lower = jnp.linalg.cholesky(diag_block)
    inverse = jax.scipy.linalg.solve_triangular(lower, identity, lower=True)
    result = lax.dot_general(
        normal_rows,
        inverse,
        (((1,), (1,)), ((), ())),
        precision=lax.Precision.HIGHEST,
        preferred_element_type=jnp.float32,
    )
    trailing = (global_rows >= first)[:, None]
    return jnp.where(trailing, result, jnp.zeros_like(result))


def solution(mesh):
    return jax.shard_map(
        body,
        mesh=mesh,
        in_specs=(P("rows", "vars"), P("vars"), P(), P()),
        out_specs=P(("rows", "vars"), None),
        check_vma=False,
    )
```

profile of v0, /device:TPU:25, one launch (start us, length us, event | category | flops | bytes accessed | tf_op | source)
XLA Modules:
  0.0 423.5 jit_solution(3627610522692604349)
XLA Ops:
  7.9 8.8 %gather_fusion = f32[512,2048]{1,0:T(8,128)} fusion(f32[1024,2048]{1,0:T(8,128)} %param.4, s32[1024]{0:T(1024)S(1)} %pad_clamp_fusion), kind=kCustom, calls=%fused_computation | custom fusion | bytes 8390656 | tf_op jit(solution)/shard_map/jit(_take)/gather | solution.py:17
  16.7 4.6 %select_multiply_fusion = f32[512,2048]{1,0:T(8,128)} fusion(f32[512,2048]{1,0:T(8,128)} %gather_fusion, f32[512]{0:T(512)S(1)} %get-tuple-element.37, pred[512]{0:T(512)(128)(4,1)S(1)} %get-tuple-element.38), kind=kLoop, calls=%fused_computation.7 | loop fusion | flops 2097152 | bytes 8391168 | tf_op jit(solution)/shard_map/mul | solution.py:17
  21.4 154.0 %all-reduce.5.cloned.1.call-done = f32[512,2048]{1,0:T(8,128)} async-done(((f32[512,2048]{1,0:T(8,128)}), f32[512,2048]{1,0:T(8,128)}) %all-reduce.5.cloned.1.call-update) | async-done | bytes 4194320 | tf_op jit(solution)/shard_map/psum | solution.py:18
  175.3 17.7 %fusion.6 = f32[1024,512]{0,1:T(8,128)} fusion(f32[1024,2048]{1,0:T(8,128)} %param.4, f32[512,2048]{1,0:T(8,128)} %all-reduce.5.cloned.1.call-done, f32[2048]{0:T(1024)S(1)} %copy-done.3), kind=kOutput, calls=%fused_computation.10 | convolution fusion | flops 12885950464 | bytes 14688256 | tf_op jit(solution)/shard_map/dot_general | solution.py:22
  193.1 7.9 %fusion = f32[512,512]{0,1:T(8,128)} fusion(f32[512,2048]{1,0:T(8,128)S(1)} %copy-done, f32[2048]{0:T(1024)S(1)} %copy-done.3), kind=kOutput, calls=%fused_computation.3 | convolution fusion | flops 6443499520 | bytes 5251072 | tf_op jit(solution)/shard_map/dot_general | solution.py:38
  201.1 0.8 iota_compare_fusion
  201.8 1.1 fusion.25
  202.9 68.5 %all-reduce.7.cloned.1.call-done = (f32[512,512]{0,1:T(8,128)}, f32[1024,512]{0,1:T(8,128)}) async-done(((f32[512,512]{0,1:T(8,128)}, f32[1024,512]{0,1:T(8,128)}), (f32[512,512]{0,1:T(8,128)}, f32[1024,512]{0,1:T(8,128)})) %all-reduce.7.cloned.1.call-update) | async-done | bytes 3145744 | tf_op jit(solution)/shard_map/psum | solution.py:45
  271.5 1.4 convert_add_fusion
  272.9 0.3 copy.8
  273.2 0.2 fusion.16
  273.5 11.7 %cholesky.104 = f32[128,128]{1,0:T(8,128)S(1)} custom-call(f32[128,128]{1,0:T(8,128)S(1)} %cholesky.266), custom_call_target="Cholesky" | custom-call | tf_op jit(solution)/shard_map/jit(cholesky)/cholesky | solution.py:46
  285.2 0.1 cholesky.224
  285.4 10.0 %custom-call.31 = f32[1,128,128]{1,2,0:T(8,128)S(1)} custom-call(f32[1,128,128]{2,1,0:T(8,128)S(1)} %get-tuple-element.34), custom_call_target="InvertDiagBlocksLowerTriangular" | custom-call | tf_op jit(solution)/shard_map/jit(cholesky)/cholesky | solution.py:46
  295.3 0.3 constant_dynamic-update-slice_fusion.3
  295.7 0.3 convolution_subtract_fusion.3
  296.0 11.7 %cholesky.217 = f32[128,128]{1,0:T(8,128)S(1)} custom-call(f32[128,128]{1,0:T(8,128)S(1)} %cholesky.270), custom_call_target="Cholesky" | custom-call | tf_op jit(solution)/shard_map/jit(cholesky)/cholesky | solution.py:46
  307.8 0.7 compare_reduce_fusion.2
  308.4 0.6 compare_reduce_fusion.3
  309.0 9.8 %custom-call.32 = f32[1,128,128]{1,2,0:T(8,128)S(1)} custom-call(f32[1,128,128]{2,1,0:T(8,128)S(1)} %get-tuple-element.31), custom_call_target="InvertDiagBlocksLowerTriangular" | custom-call | tf_op jit(solution)/shard_map/jit(cholesky)/cholesky | solution.py:46
  318.8 0.3 convolution_dynamic-update-slice_fusion
  319.1 0.4 convolution_subtract_fusion.4
  319.5 12.1 %cholesky.238 = f32[128,128]{1,0:T(8,128)S(1)} custom-call(f32[128,128]{1,0:T(8,128)S(1)} %cholesky.275), custom_call_target="Cholesky" | custom-call | tf_op jit(solution)/shard_map/jit(cholesky)/cholesky | solution.py:46
  331.6 0.7 compare_reduce_fusion.1
  332.3 9.8 %custom-call.33 = f32[1,128,128]{1,2,0:T(8,128)S(1)} custom-call(f32[1,128,128]{2,1,0:T(8,128)S(1)} %get-tuple-element.28), custom_call_target="InvertDiagBlocksLowerTriangular" | custom-call | tf_op jit(solution)/shard_map/jit(cholesky)/cholesky | solution.py:46
  342.2 0.2 convolution_dynamic-update-slice_fusion.1
  342.4 0.4 convolution_subtract_fusion.5
  342.8 11.7 %cholesky.255 = f32[128,128]{1,0:T(8,128)S(1)} custom-call(f32[128,128]{1,0:T(8,128)S(1)} %convolution_subtract_fusion.5), custom_call_target="Cholesky" | custom-call | tf_op jit(solution)/shard_map/jit(cholesky)/cholesky | solution.py:46
  354.5 0.6 compare_reduce_fusion
  357.6 0.1 select_select_fusion
  357.7 9.9 %while.1 = (s32[]{:T(128)}, f32[512,512]{1,0:T(8,128)S(1)}, s32[4,2]{0,1:T(2,128)S(1)}, f32[4,128,128]{2,1,0:T(8,128)}, s32[]{:T(128)}) while((s32[]{:T(128)}, f32[512,512]{1,0:T(8,128)S(1)}, s32[4,2]{0,1:T(2,128)S(1)}, f32[4,128,128]{2,1,0:T(8,128)}, s32[]{:T(128)}) %tuple.27), condition=%wide.while_cond, body=%wide.while_body.sunk | while | flops 2 | bytes 132705 | solution.py:47
  357.8 0.5 fusion.68
  358.3 1.9 bitcast_dynamic-update-slice_fusion.2
  360.3 0.5 fusion.68
  360.8 1.9 bitcast_dynamic-update-slice_fusion.2
  362.8 0.5 fusion.68
  363.3 1.9 bitcast_dynamic-update-slice_fusion.2
  365.2 0.5 fusion.68
  365.8 1.9 bitcast_dynamic-update-slice_fusion.2
  367.6 40.3 %custom-call.34 = f32[4,128,128]{1,2,0:T(8,128)S(1)} custom-call(f32[4,128,128]{2,1,0:T(8,128)} %get-tuple-element.12), custom_call_target="InvertDiagBlocksLowerTriangular" | custom-call | tf_op jit(solution)/shard_map/jit(_solve_triangular)/triangular_solve | solution.py:47
  407.9 1.1 fusion.30
  409.1 0.6 convolution_subtract_fusion.1
  409.7 0.4 fusion.45
  410.1 1.0 convolution_subtract_fusion
  411.1 0.4 fusion.43
  411.5 1.5 convolution_subtract_fusion.2
  413.0 0.4 fusion.42
  413.4 3.0 convolution_select_fusion
  (32 shorter events, 0.6 us)
Async XLA Ops:
  6.5 168.8 %all-reduce.5.cloned.1.call-start = ((), (), s32[]{:S(2)}) async-start(), calls=%async_computation | async-start | bytes 8388608 | tf_op jit(solution)/shard_map/psum | solution.py:18
  21.3 154.0 %copy-start.3 = (f32[2048]{0:T(1024)S(1)}, f32[2048]{0:T(1024)}, u32[]{:S(2)}) copy-start(f32[2048]{0:T(1024)} %param.5) | copy-start | bytes 24580
  21.3 250.1 %all-reduce.7.cloned.1.call-start = ((), (), s32[]{:S(2)}) async-start(), calls=%async_computation.1 | async-start | bytes 6291456 | tf_op jit(solution)/shard_map/psum | solution.py:45
  175.3 17.8 %copy-start = (f32[512,2048]{1,0:T(8,128)S(1)}, f32[512,2048]{1,0:T(8,128)}, u32[]{:S(2)}) copy-start(f32[512,2048]{1,0:T(8,128)} %all-reduce.5.cloned.1.call-done) | copy-start | bytes 12582916
  271.5 1.8 copy-start.1
  273.5 135.6 %copy-start.2 = (f32[512,512]{0,1:T(8,128)S(1)}, f32[512,512]{0,1:T(8,128)}, u32[]{:S(2)}) copy-start(f32[512,512]{0,1:T(8,128)} %fusion.25) | copy-start | bytes 3145732
Sparse Core Ops, SparseCore 0:
  21.4 153.8 all-reduce.4
  201.1 70.2 all-reduce.6
where the time goes:
time: 431 us; the launch traced here: 423 us
  waiting for transfers between devices  223 us (52%)
  other arithmetic  128 us (30%)
  matrix products  35.9 us (8%)
  local copies, waits for them, and re-layouts  19.2 us (4%)
  between operations  17.6 us (4%)
    psum x1, waiting for transfers between devices, body(): panel_rows = lax.psum(picked, 'rows')  154 us
    another operation x15, other arithmetic, body(): lower = jnp.linalg.cholesky(diag_block)  79.6 us
    psum x1, waiting for transfers between devices, body(): diag_block = lax.psum(local_block, 'vars') + identity  68.5 us
    another operation x3, other arithmetic, body(): inverse = jax.scipy.linalg.solve_triangular(lower, identity, lower=True)  40.4 us
    dot_general x1, matrix products, body(): lax.dot_general(matrix, scaled, (((1,), (1,)), ((), ())), precision=lax.P...  17.7 us
    another operation x12, local copies, waits for them, and re-layouts  9.89 us
    gather x1, local copies, waits for them, and re-layouts, body(): jnp.take(matrix, located, axis=0) * inside[:, None].astype(jnp.float32)  8.81 us
  transfers between devices with their start and end apart: 2, of which 2 were waited for; matrix products, arithmetic and copies ran while one was open for 0% of the time, Pallas kernels for 0%

commit v1 on v0

v1 whole, which is shorter than its diff:
```python
import functools
import jax
import jax.numpy as jnp
from jax import lax
from jax.experimental import pallas as pl
from jax.experimental.pallas import tpu as pltpu
from jax.sharding import PartitionSpec as P

PANEL = 512
BLK = 128
CR = 16
F32 = jnp.float32
BF16 = jnp.bfloat16
MESH = pl.DeviceIdType.MESH
NT = (((1,), (1,)), ((), ()))


def split(x):
    hi = x.astype(BF16)
    return hi, (x - hi.astype(F32)).astype(BF16)


def shifted(ref, at, count, cols):
    base = pl.multiple_of(at // 8 * 8, 8)
    wide = ref[pl.ds(base, count + 8), cols]
    turn = lax.rem(count + 8 - (at - base), count + 8)
    return pltpu.roll(wide, turn, 0)[0:count]


def dot3(ah, al, bh, bl):
    d = functools.partial(lax.dot_general, dimension_numbers=NT, preferred_element_type=F32)
    return d(ah, bh) + (d(ah, bl) + d(al, bh))


def pick_kernel(start, a_hbm, out, wide, sem):
    rows_here = a_hbm.shape[0]
    count = BLK + 8

    def base(b):
        low = jnp.clip(start[0] + b * BLK, 0, rows_here - count)
        return pl.multiple_of(low // 8 * 8, 8)

    def copy(b):
        return pltpu.make_async_copy(a_hbm.at[pl.ds(base(b), count)], wide.at[b], sem.at[b])

    for b in range(PANEL // BLK):
        copy(b).start()
    for b in range(PANEL // BLK):
        copy(b).wait()
        at = start[0] + b * BLK
        turn = lax.rem(lax.rem(base(b) - at, count) + count, count)
        row = at + lax.broadcasted_iota(jnp.int32, (BLK, 128), 0)
        inside = (row >= 0) & (row < rows_here)
        for j in range(0, a_hbm.shape[1], 128):
            part = pltpu.roll(wide[b, :, j:j + 128], turn, 0)[0:BLK]
            out[b * BLK:(b + 1) * BLK, j:j + 128] = jnp.where(inside, part, 0.0)


def panel_kernel(
    nr, nv, nred,
    own, a_hbm, bar, n_out, d_out,
    apad, ah, al, pr, pm, ph, plo, sh, sl,
    nsend, nrecv, dsend, drecv, dsum,
    a_sem, c_send, c_recv, n_ssem, n_rsem, d_ssem, d_rsem, g_ssem, g_rsem,
):
    z = lax.axis_index("rows")
    v = lax.axis_index("vars")
    rows_here = a_hbm.shape[0]
    share = rows_here // nv
    nblk = PANEL // BLK
    cpb = BLK // CR
    dr = BLK // nred
    half = rows_here // 2

    load = pltpu.make_async_copy(a_hbm, apad, a_sem)
    load.start()

    barrier = pltpu.get_barrier_semaphore()
    for i in range(1, nv):
        pl.semaphore_signal(
            barrier, inc=1, device_id={"vars": lax.rem(v + i, nv)}, device_id_type=MESH
        )

    @pl.when(z > 0)
    def _():
        pl.semaphore_signal(barrier, inc=1, device_id={"rows": z - 1}, device_id_type=MESH)

    @pl.when(z < nr - 1)
    def _():
        pl.semaphore_signal(barrier, inc=1, device_id={"rows": z + 1}, device_id_type=MESH)

    edge = jnp.where(z > 0, 1, 0) + jnp.where(z < nr - 1, 1, 0)
    pl.semaphore_wait(barrier, nv - 1 + edge)

    load.wait()

    def chunk_copy(c):
        rows = pl.ds(pl.multiple_of(c * CR, CR), CR)
        return pltpu.make_async_remote_copy(
            src_ref=pm.at[rows], dst_ref=pr.at[rows],
            send_sem=c_send.at[c], recv_sem=c_recv.at[c],
            device_id={"rows": lax.rem(z + 1, nr)}, device_id_type=MESH,
        )

    def forward(c):
        rows = pl.ds(pl.multiple_of(c * CR, CR), CR)

        @pl.when(z > 0)
        def _():
            chunk_copy(c).wait_recv()
            pm[rows, :] = own[rows, :] + pr[rows, :]

        @pl.when(z == 0)
        def _():
            pm[rows, :] = own[rows, :]

        @pl.when(z < nr - 1)
        def _():
            chunk_copy(c).start()

        val = pm[rows, :]
        hi, lo = split(val)
        ph[rows, :] = hi
        plo[rows, :] = lo
        hi, lo = split(val * bar[...])
        sh[rows, :] = hi
        sl[rows, :] = lo

    def n_copy(b, src, dst):
        return pltpu.make_async_remote_copy(
            src_ref=nsend.at[b, dst], dst_ref=nrecv.at[b, src],
            send_sem=n_ssem.at[b, dst], recv_sem=n_rsem.at[b, src],
            device_id={"vars": dst}, device_id_type=MESH,
        )

    def d_copy(b, src, dst):
        width = BLK * (b + 1)
        return pltpu.make_async_remote_copy(
            src_ref=dsend.at[b, dst, :, pl.ds(0, width)],
            dst_ref=drecv.at[b, src, :, pl.ds(0, width)],
            send_sem=d_ssem.at[b, dst], recv_sem=d_rsem.at[b, src],
            device_id={"vars": dst}, device_id_type=MESH,
        )

    def g_copy(b, src, dst):
        width = BLK * (b + 1)
        ref = dsum.at[b, src, :, pl.ds(0, width)]
        return pltpu.make_async_remote_copy(
            src_ref=ref, dst_ref=ref,
            send_sem=g_ssem.at[b, dst], recv_sem=g_rsem.at[b, src],
            device_id={"vars": dst}, device_id_type=MESH,
        )

    def others(fn, count=None):
        @pl.loop(1, nv)
        def _(i):
            fn(lax.rem(v + i, nv))

    def diag_part(b):
        rows = pl.ds(b * BLK, BLK)
        for j in range(b + 1):
            cols = pl.ds(j * BLK, BLK)
            d = dot3(sh[rows, :], sl[rows, :], ph[cols, :], plo[cols, :])
            dsend[b, :, :, cols] = d.reshape(nred, dr, BLK)

        def send(dst):
            @pl.when(dst < nred)
            def _():
                d_copy(b, v, dst).start()

        others(send)

    def diag_reduce(b):
        width = BLK * (b + 1)

        @pl.when(v < nred)
        def _():
            dsum[b, v, :, pl.ds(0, width)] = dsend[b, v, :, pl.ds(0, width)]

            def add(src):
                d_copy(b, src, v).wait_recv()
                dsum[b, v, :, pl.ds(0, width)] += drecv[b, src, :, pl.ds(0, width)]

            others(add)
            others(lambda dst: g_copy(b, v, dst).start())

    def diag_finish(b):
        width = BLK * (b + 1)

        def get(src):
            @pl.when(src < nred)
            def _():
                g_copy(b, src, v).wait_recv()

        others(get)
        if width < PANEL:
            d_out[pl.ds(b * BLK, BLK), pl.ds(width, PANEL - width)] = jnp.zeros(
                (BLK, PANEL - width), F32
            )
        d_out[pl.ds(b * BLK, BLK), pl.ds(0, width)] = dsum[b, :, :, pl.ds(0, width)].reshape(
            BLK, width
        )

    def product(b, part):
        rows = pl.ds(b * BLK, BLK)
        arows = pl.ds(part * half, half)
        n = dot3(ah[arows, :], al[arows, :], sh[rows, :], sl[rows, :])
        per = nv // 2
        nsend[b, pl.ds(part * per, per)] = n.reshape(per, share, BLK)

        @pl.loop(part * per, (part + 1) * per)
        def _(dst):
            @pl.when(dst != v)
            def _():
                n_copy(b, v, dst).start()

    def n_finish(b):
        cols = pl.ds(b * BLK, BLK)
        n_out[:, cols] = nsend[b, v]

        def add(src):
            n_copy(b, src, v).wait_recv()
            n_out[:, cols] += nrecv[b, src]

        others(add)

    per_step = rows_here // cpb
    for b in range(nblk + 1):
        if b < nblk:
            @pl.loop(0, cpb // 2)
            def _(i):
                forward(b * cpb + i)
                if b == 0:
                    for k in range(2):
                        at = (i * 2 + k) * per_step
                        hi, lo = split(apad[pl.ds(pl.multiple_of(at, per_step), per_step), :])
                        rows = pl.ds(pl.multiple_of(at, per_step), per_step)
                        ah[rows, :] = hi
                        al[rows, :] = lo
        if b > 0:
            diag_part(b - 1)
            product(b - 1, 0)
        if b < nblk:
            @pl.loop(cpb // 2, cpb)
            def _(i):
                forward(b * cpb + i)
        if b > 0:
            diag_reduce(b - 1)
            product(b - 1, 1)
        if b > 1:
            diag_finish(b - 2)
            n_finish(b - 2)
    diag_finish(nblk - 1)
    n_finish(nblk - 1)

    @pl.when(z < nr - 1)
    def _():
        @pl.loop(0, PANEL // CR)
        def _(c):
            chunk_copy(c).wait_send()

    for b in range(nblk):
        def drain(dst):
            n_copy(b, v, dst).wait_send()

            @pl.when(dst < nred)
            def _():
                d_copy(b, v, dst).wait_send()

            @pl.when(v < nred)
            def _():
                g_copy(b, v, dst).wait_send()

        others(drain)


def dot6(a, b, dims):
    return lax.dot_general(
        a, b, (dims, ((), ())), precision=lax.Precision.HIGHEST, preferred_element_type=F32
    )


def factor_kernel(share, pos, n_ref, d_ref, o_ref, lpad, ws, wm, inv):
    first_to_own = pos[0]
    nblk = PANEL // BLK
    row_id = lax.broadcasted_iota(jnp.int32, (BLK, BLK), 0)
    col_id = lax.broadcasted_iota(jnp.int32, (BLK, BLK), 1)
    eye = (row_id == col_id).astype(F32)
    lpad[...] = jnp.zeros_like(lpad)
    own_id = lax.broadcasted_iota(jnp.int32, (share, BLK), 0) + first_to_own
    below = own_id >= PANEL
    xs = []
    for b in range(nblk):
        rows = pl.ds(share + b * BLK, BLK)
        cols = slice(b * BLK, (b + 1) * BLK)
        for j in range(b):
            acc = d_ref[b * BLK:(b + 1) * BLK, j * BLK:(j + 1) * BLK]
            for i in range(j):
                acc -= dot6(
                    lpad[rows, i * BLK:(i + 1) * BLK],
                    lpad[pl.ds(share + j * BLK, BLK), i * BLK:(i + 1) * BLK],
                    ((1,), (1,)),
                )
            lpad[rows, j * BLK:(j + 1) * BLK] = dot6(acc, inv[j], ((1,), (1,)))
        acc = d_ref[b * BLK:(b + 1) * BLK, cols] + eye
        if b > 0:
            left = lpad[rows, 0:b * BLK]
            acc -= dot6(left, left, ((1,), (1,)))

        def column(k, carry):
            s, m, scale = carry
            col = jnp.sum(jnp.where(col_id == k, s, 0.0), axis=1, keepdims=True)
            ws[...] = s
            wm[...] = m
            srow = ws[pl.ds(k, 1), :]
            mrow = wm[pl.ds(k, 1), :]
            pivot = jnp.sum(jnp.where(col_id[0:1, :] == k, srow, 0.0), axis=1, keepdims=True)
            root = lax.rsqrt(pivot)
            root = root * (1.5 - 0.5 * pivot * root * root)
            low = row_id[:, 0:1] > k
            factor = jnp.where(low, col * (root * root), 0.0)
            scale = jnp.where(row_id[:, 0:1] == k, root, scale)
            return s - factor * srow, m - factor * mrow, scale

        s, m, scale = lax.fori_loop(0, BLK, column, (acc, eye, jnp.ones((BLK, 1), F32)))
        upper = jnp.where(row_id <= col_id, s, 0.0) * scale
        inv[b] = m * scale
        lpad[rows, cols] = upper.T
        x = n_ref[:, cols]
        for i in range(b):
            x -= dot6(xs[i], lpad[rows, i * BLK:(i + 1) * BLK], ((1,), (1,)))
        xs.append(dot6(x, inv[b], ((1,), (1,))))
    at = share + jnp.clip(first_to_own, -share, PANEL)
    for b in range(nblk):
        cols = slice(b * BLK, (b + 1) * BLK)
        o_ref[:, cols] = jnp.where(below, xs[b], 0.0) + shifted(lpad, at, share, cols)


def body(nr, nv, matrix, barrier, panel_index, row_offset):
    rows_here, vloc = matrix.shape
    share = rows_here // nv
    nblk = PANEL // BLK
    nred = min(nv, BLK // 8)
    dr = BLK // nred
    first = panel_index * PANEL + row_offset
    vm = pl.BlockSpec(memory_space=pltpu.VMEM)
    sm = pl.BlockSpec(memory_space=pltpu.SMEM)
    dma = pltpu.SemaphoreType.DMA
    nchunk = PANEL // CR
    picked = pl.pallas_call(
        pick_kernel,
        out_shape=jax.ShapeDtypeStruct((PANEL, vloc), F32),
        in_specs=[sm, pl.BlockSpec(memory_space=pl.ANY)],
        out_specs=vm,
        scratch_shapes=[
            pltpu.VMEM((nblk, BLK + 8, vloc), F32),
            dma((nblk,)),
        ],
        compiler_params=pltpu.CompilerParams(vmem_limit_bytes=32 << 20),
        name="pick",
    )(first - lax.axis_index("rows") * rows_here, matrix)
    n, d = pl.pallas_call(
        functools.partial(panel_kernel, nr, nv, nred),
        out_shape=(
            jax.ShapeDtypeStruct((share, PANEL), F32),
            jax.ShapeDtypeStruct((PANEL, PANEL), F32),
        ),
        in_specs=[vm, pl.BlockSpec(memory_space=pl.ANY), vm],
        out_specs=(vm, vm),
        scratch_shapes=[
            pltpu.VMEM((rows_here, vloc), F32),
            pltpu.VMEM((rows_here, vloc), BF16),
            pltpu.VMEM((rows_here, vloc), BF16),
            pltpu.VMEM((PANEL, vloc), F32),
            pltpu.VMEM((PANEL, vloc), F32),
            pltpu.VMEM((PANEL, vloc), BF16),
            pltpu.VMEM((PANEL, vloc), BF16),
            pltpu.VMEM((PANEL, vloc), BF16),
            pltpu.VMEM((PANEL, vloc), BF16),
            pltpu.VMEM((nblk, nv, share, BLK), F32),
            pltpu.VMEM((nblk, nv, share, BLK), F32),
            pltpu.VMEM((nblk, nred, dr, PANEL), F32),
            pltpu.VMEM((nblk, nv, dr, PANEL), F32),
            pltpu.VMEM((nblk, nred, dr, PANEL), F32),
            dma,
            dma((nchunk,)),
            dma((nchunk,)),
            dma((nblk, nv)),
            dma((nblk, nv)),
            dma((nblk, nv)),
            dma((nblk, nv)),
            dma((nblk, nv)),
            dma((nblk, nv)),
        ],
        compiler_params=pltpu.CompilerParams(
            collective_id=0, has_side_effects=True, vmem_limit_bytes=60 << 20
        ),
        name="panel_sums",
    )(picked, matrix, barrier.reshape(1, vloc))
    own = lax.axis_index("rows") * rows_here + lax.axis_index("vars") * share
    return pl.pallas_call(
        functools.partial(factor_kernel, share),
        out_shape=jax.ShapeDtypeStruct((share, PANEL), F32),
        in_specs=[sm, vm, vm],
        out_specs=vm,
        scratch_shapes=[
            pltpu.VMEM((PANEL + 2 * share + 8, PANEL), F32),
            pltpu.VMEM((BLK, BLK), F32),
            pltpu.VMEM((BLK, BLK), F32),
            pltpu.VMEM((nblk, BLK, BLK), F32),
        ],
        compiler_params=pltpu.CompilerParams(vmem_limit_bytes=32 << 20),
        name="factor",
    )(own - first, n, d)


def solution(mesh):
    return jax.shard_map(
        functools.partial(body, mesh.shape["rows"], mesh.shape["vars"]),
        mesh=mesh,
        in_specs=(P("rows", "vars"), P("vars"), P(), P()),
        out_specs=P(("rows", "vars"), None),
        check_vma=False,
    )
```

time: 431 us -> 216 us (0.50); the launches traced: 423 us -> 215 us
  waiting for transfers between devices: 223 us -> 0 us
  Pallas kernels: 0 us -> 206 us
  other arithmetic: 128 us -> 0 us
  matrix products: 35.9 us -> 0 us
  between operations: 17.6 us -> 1.34 us
  local copies, waits for them, and re-layouts: 19.2 us -> 7.47 us
    psum x2 -> x0, waiting for transfers between devices: 222 us -> none  [the longest x1 154 us: body(): panel_rows = lax.psum(picked, 'rows')]
    pallas_call x0 -> x3, Pallas kernels: none -> 206 us  [the longest x1 131 us: body(): pl.pallas_call(functools.partial(panel_kernel, nr, nv, nred), out_shape=(...]
    another operation x18 -> x0, other arithmetic: 120 us -> none  [the longest x15 79.6 us: body(): lower = jnp.linalg.cholesky(diag_block)]
    dot_general x3 -> x0, matrix products: 28.6 us -> none  [the longest x1 17.7 us: body(): lax.dot_general(matrix, scaled, (((1,), (1,)), ((), ())), precision=lax.P...]
    another operation x17 -> x0, local copies, waits for them, and re-layouts: 10 us -> none
    gather x1 -> x0, local copies, waits for them, and re-layouts: 8.81 us -> none  [body(): jnp.take(matrix, located, axis=0) * inside[:, None].astype(jnp.float32)]
    unnamed x8, local copies, waits for them, and re-layouts: 0.02 us -> 7.47 us
    another operation x13 -> x0, matrix products: 7.29 us -> none  [the longest x7 5.43 us: body(): inverse = jax.scipy.linalg.solve_triangular(lower, identity, lower=True)]
  transfers between devices with their start and end apart: 2 -> 0, of which waited for: 2 -> 0; matrix products, arithmetic and copies ran while one was open for 0% -> 0% of each run, Pallas kernels for 0% -> 0%
where the time goes in v1:
time: 216 us; the launch traced here: 215 us
  Pallas kernels  206 us (95%)
  local copies, waits for them, and re-layouts  7.47 us (3%)
    pallas_call x1, Pallas kernels, body(): pl.pallas_call(functools.partial(panel_kernel, nr, nv, nred), out_shape=(...  131 us
    pallas_call x1, Pallas kernels, body(): pl.pallas_call(functools.partial(factor_kernel, share), out_shape=jax.Sha...  71.3 us
    unnamed x8, local copies, waits for them, and re-layouts  7.47 us

profile of v1, /device:TPU:25, one launch (start us, length us, event | category | flops | bytes accessed | tf_op | source)
XLA Modules:
  0.0 214.5 jit_solution(557939040044276901)
XLA Ops:
  1.3 0.0 copy-start
  1.3 3.4 %copy-done = f32[1024,2048]{1,0:T(8,128)S(1)} copy-done((f32[1024,2048]{1,0:T(8,128)S(1)}, f32[1024,2048]{1,0:T(8,128)}, u32[]{:S(2)}) %copy-start) | copy-done | bytes 8388632
  4.7 3.1 %pick.1.own = f32[512,2048]{1,0:T(8,128)S(1)} custom-call(s32[1]{0:T(128)S(6)} %sub.15.start, f32[1024,2048]{1,0:T(8,128)S(1)} %copy-done), custom_call_target="tpu_custom_call" | custom-call | tf_op jit(solution)/shard_map/pick/pallas_call | solution.py:350
  7.8 0.0 copy-start.1
  7.8 1.9 copy-done.1
  9.7 131.4 %panel_sums.1 = (f32[128,512]{1,0:T(8,128)}, f32[512,512]{1,0:T(8,128)}) custom-call(f32[512,2048]{1,0:T(8,128)} %copy-done.1, f32[1024,2048]{1,0:T(8,128)} %a_hbm.3, f32[1,2048]{1,0:T(1,128)} %bitcast.3), custom_call_target="tpu_custom_call" | custom-call | tf_op jit(solution)/shard_map/panel_sums/pallas_call | solution.py:362
  141.1 0.0 copy-start.2
  141.1 1.2 copy-done.2
  142.3 0.0 copy-start.3
  142.3 0.9 copy-done.3
  143.3 71.3 %factor.1 = f32[128,512]{1,0:T(8,128)} custom-call(s32[1]{0:T(128)S(6)} %sub.13.pos, f32[128,512]{1,0:T(8,128)S(1)} %copy-done.3, f32[512,512]{1,0:T(8,128)S(1)} %copy-done.2), custom_call_target="tpu_custom_call" | custom-call | tf_op jit(solution)/shard_map/factor/pallas_call | solution.py:401
Async XLA Ops:
  1.3 3.4 %copy-start = (f32[1024,2048]{1,0:T(8,128)S(1)}, f32[1024,2048]{1,0:T(8,128)}, u32[]{:S(2)}) copy-start(f32[1024,2048]{1,0:T(8,128)} %a_hbm.3) | copy-start | bytes 25165828
  7.8 1.9 copy-start.1
  141.1 1.2 copy-start.2
  142.3 0.9 copy-start.3

commit v2 on v1

--- a/solution.py
+++ b/solution.py
@@ -9,6 +9,7 @@
 PANEL = 512
 BLK = 128
 CR = 16
+GRP = 16
 F32 = jnp.float32
 BF16 = jnp.bfloat16
 MESH = pl.DeviceIdType.MESH
@@ -30,6 +31,71 @@
 def dot3(ah, al, bh, bl):
     d = functools.partial(lax.dot_general, dimension_numbers=NT, preferred_element_type=F32)
     return d(ah, bh) + (d(ah, bl) + d(al, bh))
+
+
+def dot6(a, b, dims):
+    return lax.dot_general(
+        a, b, (dims, ((), ())), precision=lax.Precision.HIGHEST, preferred_element_type=F32
+    )
+
+
+def eliminate(k, ws, wm):
+    rows = pl.ds(pl.multiple_of(k, GRP), GRP)
+    s = ws[rows, :]
+    m = wm[rows, :]
+    turned = pltpu.roll(s, lax.rem(BLK - k, BLK), 1)
+    cols = [jnp.broadcast_to(turned[:, t:t + 1], (GRP, BLK)) for t in range(GRP)]
+    row_id = lax.broadcasted_iota(jnp.int32, (GRP, BLK), 0)
+    lane_id = lax.broadcasted_iota(jnp.int32, (GRP, BLK), 1)
+    root = jnp.ones((GRP, BLK), F32)
+    for t in range(GRP):
+        pivot = cols[t][t:t + 1, :]
+        r = lax.rsqrt(pivot)
+        r = r * (1.5 - 0.5 * pivot * r * r)
+        rr = r * r
+        factor = jnp.where(row_id > t, cols[t] * rr, 0.0)
+        root = jnp.where(row_id == t, r, root)
+        for u in range(t + 1, GRP):
+            cols[u] = cols[u] - factor * cols[u][t:t + 1, :]
+        s = s - factor * s[t:t + 1, :]
+        m = m - factor * m[t:t + 1, :]
+    s = jnp.where(lane_id >= k, s * root, 0.0)
+    m = m * root
+    ws[...] -= dot6(s, s, ((0,), (0,)))
+    wm[...] -= dot6(s, m, ((0,), (0,)))
+    ws[rows, :] = s
+    wm[rows, :] = m
+
+
+def factor_start(b, diag, lower, inv, ws, wm):
+    rows = pl.ds(b * BLK, BLK)
+    row_id = lax.broadcasted_iota(jnp.int32, (BLK, BLK), 0)
+    col_id = lax.broadcasted_iota(jnp.int32, (BLK, BLK), 1)
+    eye = (row_id == col_id).astype(F32)
+    for j in range(b):
+        cols = pl.ds(j * BLK, BLK)
+        acc = diag(j)
+        if j > 0:
+            left = pl.ds(0, j * BLK)
+            acc -= dot6(lower[rows, left], lower[cols, left], ((1,), (1,)))
+        lower[rows, cols] = dot6(acc, inv[j], ((1,), (1,)))
+    acc = diag(b) + eye
+    if b > 0:
+        left = lower[rows, 0:b * BLK]
+        acc -= dot6(left, left, ((1,), (1,)))
+    ws[...] = acc
+    wm[...] = eye
+
+
+def factor_end(b, lower, inv, ws, wm):
+    rows = pl.ds(b * BLK, BLK)
+    row_id = lax.broadcasted_iota(jnp.int32, (BLK, BLK), 0)
+    col_id = lax.broadcasted_iota(jnp.int32, (BLK, BLK), 1)
+    inv[b] = wm[...]
+    lower[rows, pl.ds(b * BLK, BLK)] = jnp.where(row_id <= col_id, ws[...], 0.0).T
+    rest = PANEL - (b + 1) * BLK
+    if rest > 0:
+        lower[rows, pl.ds((b + 1) * BLK, rest)] = jnp.zeros((BLK, rest), F32)
 
 
 def pick_kernel(start, a_hbm, out, wide, sem):
@@ -58,9 +124,9 @@
 
 def panel_kernel(
     nr, nv, nred,
-    own, a_hbm, bar, n_out, d_out,
+    own, a_hbm, bar, x_out, lower,
     apad, ah, al, pr, pm, ph, plo, sh, sl,
-    nsend, nrecv, dsend, drecv, dsum,
+    nsend, nrecv, dsend, drecv, dsum, ws, wm, inv,
     a_sem, c_send, c_recv, n_ssem, n_rsem, d_ssem, d_rsem, g_ssem, g_rsem,
 ):
     z = lax.axis_index("rows")
@@ -185,21 +251,17 @@
             others(lambda dst: g_copy(b, v, dst).start())
 
     def diag_finish(b):
-        width = BLK * (b + 1)
-
         def get(src):
             @pl.when(src < nred)
             def _():
                 g_copy(b, src, v).wait_recv()
 
         others(get)
-        if width < PANEL:
-            d_out[pl.ds(b * BLK, BLK), pl.ds(width, PANEL - width)] = jnp.zeros(
-                (BLK, PANEL - width), F32
-            )
-        d_out[pl.ds(b * BLK, BLK), pl.ds(0, width)] = dsum[b, :, :, pl.ds(0, width)].reshape(
-            BLK, width
-        )
+
+        def diag(j):
+            return dsum[b, :, :, pl.ds(j * BLK, BLK)].reshape(BLK, BLK)
+
+        factor_start(b, diag, lower, inv, ws, wm)
 
     def product(b, part):
         rows = pl.ds(b * BLK, BLK)
@@ -214,44 +276,56 @@
             def _():
                 n_copy(b, v, dst).start()
 
-    def n_finish(b):
-        cols = pl.ds(b * BLK, BLK)
-        n_out[:, cols] = nsend[b, v]
-
+    def solve(b):
         def add(src):
             n_copy(b, src, v).wait_recv()
-            n_out[:, cols] += nrecv[b, src]
+            nsend[b, v] += nrecv[b, src]
 
         others(add)
+        x = nsend[b, v]
+        if b > 0:
+            left = pl.ds(0, b * BLK)
+            x -= dot6(x_out[:, left], lower[pl.ds(b * BLK, BLK), left], ((1,), (1,)))
+        x_out[:, pl.ds(b * BLK, BLK)] = dot6(x, inv[b], ((1,), (1,)))
+
+    def steps(b, low, high, also=None):
+        @pl.loop(low, high)
+        def _(i):
+            if b < nblk:
+                forward(b * cpb + i)
+            if also is not None:
+                also(i)
+
+    def halves(i):
+        for k in range(2):
+            at = pl.multiple_of((i * 2 + k) * per_step, per_step)
+            rows = pl.ds(at, per_step)
+            hi, lo = split(apad[rows, :])
+            ah[rows, :] = hi
+            al[rows, :] = lo
 
     per_step = rows_here // cpb
-    for b in range(nblk + 1):
-        if b < nblk:
-            @pl.loop(0, cpb // 2)
-            def _(i):
-                forward(b * cpb + i)
-                if b == 0:
-                    for k in range(2):
-                        at = (i * 2 + k) * per_step
-                        hi, lo = split(apad[pl.ds(pl.multiple_of(at, per_step), per_step), :])
-                        rows = pl.ds(pl.multiple_of(at, per_step), per_step)
-                        ah[rows, :] = hi
-                        al[rows, :] = lo
-        if b > 0:
-            diag_part(b - 1)
-            product(b - 1, 0)
-        if b < nblk:
-            @pl.loop(cpb // 2, cpb)
-            def _(i):
-                forward(b * cpb + i)
-        if b > 0:
-            diag_reduce(b - 1)
-            product(b - 1, 1)
-        if b > 1:
-            diag_finish(b - 2)
-            n_finish(b - 2)
-    diag_finish(nblk - 1)
-    n_finish(nblk - 1)
+    mid = cpb // 2
+    groups = BLK // GRP // (cpb - mid)
+    steps(0, 0, mid, halves)
+    steps(0, mid, cpb)
+    for b in range(1, nblk + 1):
+        diag_part(b - 1)
+        steps(b, 0, 2)
+        product(b - 1, 0)
+        steps(b, 2, 3)
+        diag_reduce(b - 1)
+        steps(b, 3, mid)
+        product(b - 1, 1)
+        diag_finish(b - 1)
+
+        def columns(i):
+            for g in range(groups):
+                eliminate(((i - mid) * groups + g) * GRP, ws, wm)
+
+        steps(b, mid, cpb, columns)
+        factor_end(b - 1, lower, inv, ws, wm)
+        solve(b - 1)
 
     @pl.when(z < nr - 1)
     def _():
@@ -274,66 +348,20 @@
         others(drain)
 
 
-def dot6(a, b, dims):
-    return lax.dot_general(
-        a, b, (dims, ((), ())), precision=lax.Precision.HIGHEST, preferred_element_type=F32
-    )
-
-
-def factor_kernel(share, pos, n_ref, d_ref, o_ref, lpad, ws, wm, inv):
-    first_to_own = pos[0]
-    nblk = PANEL // BLK
-    row_id = lax.broadcasted_iota(jnp.int32, (BLK, BLK), 0)
-    col_id = lax.broadcasted_iota(jnp.int32, (BLK, BLK), 1)
-    eye = (row_id == col_id).astype(F32)
-    lpad[...] = jnp.zeros_like(lpad)
-    own_id = lax.broadcasted_iota(jnp.int32, (share, BLK), 0) + first_to_own
-    below = own_id >= PANEL
-    xs = []
-    for b in range(nblk):
-        rows = pl.ds(share + b * BLK, BLK)
-        cols = slice(b * BLK, (b + 1) * BLK)
-        for j in range(b):
-            acc = d_ref[b * BLK:(b + 1) * BLK, j * BLK:(j + 1) * BLK]
-            for i in range(j):
-                acc -= dot6(
-                    lpad[rows, i * BLK:(i + 1) * BLK],
-                    lpad[pl.ds(share + j * BLK, BLK), i * BLK:(i + 1) * BLK],
-                    ((1,), (1,)),
-                )
-            lpad[rows, j * BLK:(j + 1) * BLK] = dot6(acc, inv[j], ((1,), (1,)))
-        acc = d_ref[b * BLK:(b + 1) * BLK, cols] + eye
-        if b > 0:
-            left = lpad[rows, 0:b * BLK]
-            acc -= dot6(left, left, ((1,), (1,)))
-
-        def column(k, carry):
-            s, m, scale = carry
-            col = jnp.sum(jnp.where(col_id == k, s, 0.0), axis=1, keepdims=True)
-            ws[...] = s
-            wm[...] = m
-            srow = ws[pl.ds(k, 1), :]
-            mrow = wm[pl.ds(k, 1), :]
-            pivot = jnp.sum(jnp.where(col_id[0:1, :] == k, srow, 0.0), axis=1, keepdims=True)
-            root = lax.rsqrt(pivot)
-            root = root * (1.5 - 0.5 * pivot * root * root)
-            low = row_id[:, 0:1] > k
-            factor = jnp.where(low, col * (root * root), 0.0)
-            scale = jnp.where(row_id[:, 0:1] == k, root, scale)
-            return s - factor * srow, m - factor * mrow, scale
-
-        s, m, scale = lax.fori_loop(0, BLK, column, (acc, eye, jnp.ones((BLK, 1), F32)))
-        upper = jnp.where(row_id <= col_id, s, 0.0) * scale
-        inv[b] = m * scale
-        lpad[rows, cols] = upper.T
-        x = n_ref[:, cols]
-        for i in range(b):
-            x -= dot6(xs[i], lpad[rows, i * BLK:(i + 1) * BLK], ((1,), (1,)))
-        xs.append(dot6(x, inv[b], ((1,), (1,))))
-    at = share + jnp.clip(first_to_own, -share, PANEL)
-    for b in range(nblk):
-        cols = slice(b * BLK, (b + 1) * BLK)
-        o_ref[:, cols] = jnp.where(below, xs[b], 0.0) + shifted(lpad, at, share, cols)
+def finish_kernel(share, pos, x_ref, l_hbm, o_ref, wide, sem):
+    count = share + 8
+    low = jnp.clip(pos[0], 0, PANEL - count)
+    base = pl.multiple_of(low // 8 * 8, 8)
+    copy = pltpu.make_async_copy(l_hbm.at[pl.ds(base, count)], wide, sem)
+    copy.start()
+    copy.wait()
+    turn = lax.rem(lax.rem(base - pos[0], count) + count, count)
+    row = pos[0] + lax.broadcasted_iota(jnp.int32, (share, 128), 0)
+    inside = (row >= 0) & (row < PANEL)
+    for j in range(0, PANEL, 128):
+        part = pltpu.roll(wide[:, j:j + 128], turn, 0)[0:share]
+        x = jnp.where(row >= PANEL, x_ref[:, j:j + 128], 0.0)
+        o_ref[:, j:j + 128] = jnp.where(inside, part, x)
 
 
 def body(nr, nv, matrix, barrier, panel_index, row_offset):
@@ -359,7 +387,7 @@
         compiler_params=pltpu.CompilerParams(vmem_limit_bytes=32 << 20),
         name="pick",
     )(first - lax.axis_index("rows") * rows_here, matrix)
-    n, d = pl.pallas_call(
+    x, low = pl.pallas_call(
         functools.partial(panel_kernel, nr, nv, nred),
         out_shape=(
             jax.ShapeDtypeStruct((share, PANEL), F32),
@@ -382,6 +410,9 @@
             pltpu.VMEM((nblk, nred, dr, PANEL), F32),
             pltpu.VMEM((nblk, nv, dr, PANEL), F32),
             pltpu.VMEM((nblk, nred, dr, PANEL), F32),
+            pltpu.VMEM((BLK, BLK), F32),
+            pltpu.VMEM((BLK, BLK), F32),
+            pltpu.VMEM((nblk, BLK, BLK), F32),
             dma,
             dma((nchunk,)),
             dma((nchunk,)),
@@ -399,19 +430,13 @@
     )(picked, matrix, barrier.reshape(1, vloc))
     own = lax.axis_index("rows") * rows_here + lax.axis_index("vars") * share
     return pl.pallas_call(
-        functools.partial(factor_kernel, share),
+        functools.partial(finish_kernel, share),
         out_shape=jax.ShapeDtypeStruct((share, PANEL), F32),
-        in_specs=[sm, vm, vm],
+        in_specs=[sm, vm, pl.BlockSpec(memory_space=pl.ANY)],
         out_specs=vm,
-        scratch_shapes=[
-            pltpu.VMEM((PANEL + 2 * share + 8, PANEL), F32),
-            pltpu.VMEM((BLK, BLK), F32),
-            pltpu.VMEM((BLK, BLK), F32),
-            pltpu.VMEM((nblk, BLK, BLK), F32),
-        ],
-        compiler_params=pltpu.CompilerParams(vmem_limit_bytes=32 << 20),
-        name="factor",
-    )(own - first, n, d)
+        scratch_shapes=[pltpu.VMEM((share + 8, PANEL), F32), dma],
+        name="finish",
+    )(own - first, x, low)
 
 
 def solution(mesh):

time: 216 us -> 155 us (0.72)
  Pallas kernels: 206 us -> 148 us
  local copies, waits for them, and re-layouts: 7.47 us -> 5.3 us
    pallas_call x1, Pallas kernels: 71.3 us -> 2.78 us  [body(): pl.pallas_call(functools.partial(finish_kernel, share), out_shape=jax.Sha...]
    pallas_call x1, Pallas kernels: 131 us -> 142 us  [body(): pl.pallas_call(functools.partial(panel_kernel, nr, nv, nred), out_shape=(...]
    unnamed x8 -> x4, local copies, waits for them, and re-layouts: 7.47 us -> 5.3 us
where the time goes in v2:
time: 155 us
  Pallas kernels  148 us (95%)
  local copies, waits for them, and re-layouts  5.3 us (3%)
    pallas_call x1, Pallas kernels, body(): pl.pallas_call(functools.partial(panel_kernel, nr, nv, nred), out_shape=(...  142 us
    unnamed x4, local copies, waits for them, and re-layouts  5.3 us
    pallas_call x1, Pallas kernels, body(): pl.pallas_call(pick_kernel, out_shape=jax.ShapeDtypeStruct((PANEL, vloc),...  3.11 us

profile of v2, /device:TPU:25, one launch (start us, length us, event | category | flops | bytes accessed | tf_op | source)
XLA Modules:
  0.0 154.7 jit_solution(14033237502543310722)
XLA Ops:
  1.3 0.0 copy-start
  1.3 3.4 %copy-done = f32[1024,2048]{1,0:T(8,128)S(1)} copy-done((f32[1024,2048]{1,0:T(8,128)S(1)}, f32[1024,2048]{1,0:T(8,128)}, u32[]{:S(2)}) %copy-start) | copy-done | bytes 8388632
  4.7 3.1 %pick.1.own = f32[512,2048]{1,0:T(8,128)S(1)} custom-call(s32[1]{0:T(128)S(6)} %sub.15.start, f32[1024,2048]{1,0:T(8,128)S(1)} %copy-done), custom_call_target="tpu_custom_call" | custom-call | tf_op jit(solution)/shard_map/pick/pallas_call | solution.py:378
  7.8 0.0 copy-start.1
  7.8 1.9 %copy-done.1 = f32[512,2048]{1,0:T(8,128)} copy-done((f32[512,2048]{1,0:T(8,128)}, f32[512,2048]{1,0:T(8,128)S(1)}, u32[]{:S(2)}) %copy-start.1) | copy-done | bytes 4194328
  9.7 142.0 %panel_sums.1 = (f32[128,512]{1,0:T(8,128)}, f32[512,512]{1,0:T(8,128)}) custom-call(f32[512,2048]{1,0:T(8,128)} %copy-done.1, f32[1024,2048]{1,0:T(8,128)} %a_hbm.3, f32[1,2048]{1,0:T(1,128)} %bitcast.3), custom_call_target="tpu_custom_call" | custom-call | tf_op jit(solution)/shard_map/panel_sums/pallas_call | solution.py:390
  151.8 2.8 %finish.1 = f32[128,512]{1,0:T(8,128)} custom-call(s32[1]{0:T(128)S(6)} %sub.13.pos, f32[128,512]{1,0:T(8,128)} %get-tuple-element.7.x_ref, f32[512,512]{1,0:T(8,128)} %get-tuple-element.8.l_hbm), custom_call_target="tpu_custom_call" | custom-call | tf_op jit(solution)/shard_map/finish/pallas_call | solution.py:432
Async XLA Ops:
  1.3 3.4 %copy-start = (f32[1024,2048]{1,0:T(8,128)S(1)}, f32[1024,2048]{1,0:T(8,128)}, u32[]{:S(2)}) copy-start(f32[1024,2048]{1,0:T(8,128)} %a_hbm.3) | copy-start | bytes 25165828
  7.8 1.9 %copy-start.1 = (f32[512,2048]{1,0:T(8,128)}, f32[512,2048]{1,0:T(8,128)S(1)}, u32[]{:S(2)}) copy-start(f32[512,2048]{1,0:T(8,128)S(1)} %pick.1.own) | copy-start | bytes 12582916

commit v3 on v2

--- a/solution.py
+++ b/solution.py
@@ -21,16 +21,8 @@
     return hi, (x - hi.astype(F32)).astype(BF16)
 
 
-def shifted(ref, at, count, cols):
-    base = pl.multiple_of(at // 8 * 8, 8)
-    wide = ref[pl.ds(base, count + 8), cols]
-    turn = lax.rem(count + 8 - (at - base), count + 8)
-    return pltpu.roll(wide, turn, 0)[0:count]
-
-
-def dot3(ah, al, bh, bl):
-    d = functools.partial(lax.dot_general, dimension_numbers=NT, preferred_element_type=F32)
-    return d(ah, bh) + (d(ah, bl) + d(al, bh))
+def dot(a, b):
+    return lax.dot_general(a, b, NT, preferred_element_type=F32)
 
 
 def dot6(a, b, dims):
@@ -125,9 +117,9 @@
 def panel_kernel(
     nr, nv, nred,
     own, a_hbm, bar, x_out, lower,
-    apad, ah, al, pr, pm, ph, plo, sh, sl,
+    apad, ah, al, pr, pm, ph, plo, sc,
     nsend, nrecv, dsend, drecv, dsum, ws, wm, inv,
-    a_sem, c_send, c_recv, n_ssem, n_rsem, d_ssem, d_rsem, g_ssem, g_rsem,
+    a_sem, o_sem, c_send, c_recv, n_ssem, n_rsem, d_ssem, d_rsem, g_ssem, g_rsem,
 ):
     z = lax.axis_index("rows")
     v = lax.axis_index("vars")
@@ -141,6 +133,13 @@
     load = pltpu.make_async_copy(a_hbm, apad, a_sem)
     load.start()
 
+    def own_copy(b):
+        rows = pl.ds(b * BLK, BLK)
+        return pltpu.make_async_copy(own.at[rows], pm.at[rows], o_sem.at[b])
+
+    for b in range(nblk):
+        own_copy(b).start()
+
     barrier = pltpu.get_barrier_semaphore()
     for i in range(1, nv):
         pl.semaphore_signal(
@@ -158,7 +157,6 @@
     edge = jnp.where(z > 0, 1, 0) + jnp.where(z < nr - 1, 1, 0)
     pl.semaphore_wait(barrier, nv - 1 + edge)
 
-    load.wait()
 
     def chunk_copy(c):
         rows = pl.ds(pl.multiple_of(c * CR, CR), CR)
@@ -168,17 +166,14 @@
             device_id={"rows": lax.rem(z + 1, nr)}, device_id_type=MESH,
         )
 
-    def forward(c):
+    def forward(b, i):
+        c = b * cpb + i
         rows = pl.ds(pl.multiple_of(c * CR, CR), CR)
 
         @pl.when(z > 0)
         def _():
             chunk_copy(c).wait_recv()
-            pm[rows, :] = own[rows, :] + pr[rows, :]
-
-        @pl.when(z == 0)
-        def _():
-            pm[rows, :] = own[rows, :]
+            pm[rows, :] = pm[rows, :] + pr[rows, :]
 
         @pl.when(z < nr - 1)
         def _():
@@ -189,8 +184,8 @@
         ph[rows, :] = hi
         plo[rows, :] = lo
         hi, lo = split(val * bar[...])
-        sh[rows, :] = hi
-        sl[rows, :] = lo
+        sc[b, pl.ds(pl.multiple_of(i * CR, CR), CR), :] = hi
+        sc[b, pl.ds(pl.multiple_of(BLK + i * CR, CR), CR), :] = lo
 
     def n_copy(b, src, dst):
         return pltpu.make_async_remote_copy(
@@ -223,11 +218,10 @@
             fn(lax.rem(v + i, nv))
 
     def diag_part(b):
-        rows = pl.ds(b * BLK, BLK)
-        for j in range(b + 1):
-            cols = pl.ds(j * BLK, BLK)
-            d = dot3(sh[rows, :], sl[rows, :], ph[cols, :], plo[cols, :])
-            dsend[b, :, :, cols] = d.reshape(nred, dr, BLK)
+        width = BLK * (b + 1)
+        d = dot(sc[b], ph[pl.ds(0, width), :])
+        d = d[:BLK] + (d[BLK:] + dot(sc[b, pl.ds(0, BLK), :], plo[pl.ds(0, width), :]))
+        dsend[b, :, :, pl.ds(0, width)] = d.reshape(nred, dr, width)
 
         def send(dst):
             @pl.when(dst < nred)
@@ -264,9 +258,9 @@
         factor_start(b, diag, lower, inv, ws, wm)
 
     def product(b, part):
-        rows = pl.ds(b * BLK, BLK)
         arows = pl.ds(part * half, half)
-        n = dot3(ah[arows, :], al[arows, :], sh[rows, :], sl[rows, :])
+        n = dot(ah[arows, :], sc[b])
+        n = n[:, :BLK] + (n[:, BLK:] + dot(al[arows, :], sc[b, pl.ds(0, BLK), :]))
         per = nv // 2
         nsend[b, pl.ds(part * per, per)] = n.reshape(per, share, BLK)
 
@@ -292,13 +286,13 @@
         @pl.loop(low, high)
         def _(i):
             if b < nblk:
-                forward(b * cpb + i)
+                forward(b, i)
             if also is not None:
                 also(i)
 
     def halves(i):
         for k in range(2):
-            at = pl.multiple_of((i * 2 + k) * per_step, per_step)
+            at = pl.multiple_of(((i - mid) * 2 + k) * per_step, per_step)
             rows = pl.ds(at, per_step)
             hi, lo = split(apad[rows, :])
             ah[rows, :] = hi
@@ -307,9 +301,13 @@
     per_step = rows_here // cpb
     mid = cpb // 2
     groups = BLK // GRP // (cpb - mid)
-    steps(0, 0, mid, halves)
-    steps(0, mid, cpb)
+    own_copy(0).wait()
+    steps(0, 0, mid)
+    load.wait()
+    steps(0, mid, cpb, halves)
     for b in range(1, nblk + 1):
+        if b < nblk:
+            own_copy(b).wait()
         diag_part(b - 1)
         steps(b, 0, 2)
         product(b - 1, 0)
@@ -384,7 +382,7 @@
             pltpu.VMEM((nblk, BLK + 8, vloc), F32),
             dma((nblk,)),
         ],
-        compiler_params=pltpu.CompilerParams(vmem_limit_bytes=32 << 20),
+        compiler_params=pltpu.CompilerParams(vmem_limit_bytes=58 << 20),
         name="pick",
     )(first - lax.axis_index("rows") * rows_here, matrix)
     x, low = pl.pallas_call(
@@ -393,7 +391,7 @@
             jax.ShapeDtypeStruct((share, PANEL), F32),
             jax.ShapeDtypeStruct((PANEL, PANEL), F32),
         ),
-        in_specs=[vm, pl.BlockSpec(memory_space=pl.ANY), vm],
+        in_specs=[pl.BlockSpec(memory_space=pl.ANY), pl.BlockSpec(memory_space=pl.ANY), vm],
         out_specs=(vm, vm),
         scratch_shapes=[
             pltpu.VMEM((rows_here, vloc), F32),
@@ -403,8 +401,7 @@
             pltpu.VMEM((PANEL, vloc), F32),
             pltpu.VMEM((PANEL, vloc), BF16),
             pltpu.VMEM((PANEL, vloc), BF16),
-            pltpu.VMEM((PANEL, vloc), BF16),
-            pltpu.VMEM((PANEL, vloc), BF16),
+            pltpu.VMEM((nblk, 2 * BLK, vloc), BF16),
             pltpu.VMEM((nblk, nv, share, BLK), F32),
             pltpu.VMEM((nblk, nv, share, BLK), F32),
             pltpu.VMEM((nblk, nred, dr, PANEL), F32),
@@ -414,6 +411,7 @@
             pltpu.VMEM((BLK, BLK), F32),
             pltpu.VMEM((nblk, BLK, BLK), F32),
             dma,
+            dma((nblk,)),
             dma((nchunk,)),
             dma((nchunk,)),
             dma((nblk, nv)),

time: 155 us -> 145 us (0.935)
  local copies, waits for them, and re-layouts: 5.3 us -> 0 us
  Pallas kernels: 148 us -> 143 us
    pallas_call x1, Pallas kernels: 142 us -> 135 us  [body(): pl.pallas_call(functools.partial(panel_kernel, nr, nv, nred), out_shape=(...]
    unnamed x4 -> x0, local copies, waits for them, and re-layouts: 5.3 us -> none
    pallas_call x1, Pallas kernels: 3.11 us -> 5.6 us  [body(): pl.pallas_call(pick_kernel, out_shape=jax.ShapeDtypeStruct((PANEL, vloc),...]
where the time goes in v3:
time: 145 us; the launch traced here: 144 us
  Pallas kernels  143 us (99%)
  between operations  1.48 us (1%)
    pallas_call x1, Pallas kernels, body(): pl.pallas_call(functools.partial(panel_kernel, nr, nv, nred), out_shape=(...  135 us
    pallas_call x1, Pallas kernels, body(): pl.pallas_call(pick_kernel, out_shape=jax.ShapeDtypeStruct((PANEL, vloc),...  5.6 us

profile of v3, /device:TPU:25, one launch (start us, length us, event | category | flops | bytes accessed | tf_op | source)
XLA Modules:
  0.0 144.4 jit_solution(3810091050107738725)
XLA Ops:
  1.3 5.6 %pick.1.own = f32[512,2048]{1,0:T(8,128)} custom-call(s32[1]{0:T(128)S(6)} %sub.15.start, f32[1024,2048]{1,0:T(8,128)} %a_hbm.3), custom_call_target="tpu_custom_call" | custom-call | tf_op jit(solution)/shard_map/pick/pallas_call | solution.py:376
  6.9 134.5 %panel_sums.1 = (f32[128,512]{1,0:T(8,128)}, f32[512,512]{1,0:T(8,128)}) custom-call(f32[512,2048]{1,0:T(8,128)} %pick.1.own, f32[1024,2048]{1,0:T(8,128)} %a_hbm.3, f32[1,2048]{1,0:T(1,128)} %bitcast.3), custom_call_target="tpu_custom_call" | custom-call | tf_op jit(solution)/shard_map/panel_sums/pallas_call | solution.py:388
  141.4 2.8 %finish.1 = f32[128,512]{1,0:T(8,128)} custom-call(s32[1]{0:T(128)S(6)} %sub.13.pos, f32[128,512]{1,0:T(8,128)} %get-tuple-element.7.x_ref, f32[512,512]{1,0:T(8,128)} %get-tuple-element.8.l_hbm), custom_call_target="tpu_custom_call" | custom-call | tf_op jit(solution)/shard_map/finish/pallas_call | solution.py:430
